TPU v7x, 32 devices: a whole 2x2x4 slice. The times are simulated.
32 devices in a mesh: groups: 2 (over x), branch: 4 (over y, core), head: 4 (over z).
Axes of the slice: x: 2, y: 2, z: 4, core: 2. Of those that a mesh axis runs over, the one named last changes fastest.
Arguments:
- queries: bfloat16 [128, 8192], P(('groups', 'branch'), 'head'), parts along dimension 0, may hold values from -100 to 100, as said below
- root_keys: bfloat16 [32768, 1024], P(('groups', 'branch'), 'head'), parts along dimension 0, may hold values from -6 to 6
- root_values: bfloat16 [32768, 1024], P(('groups', 'branch'), 'head'), parts along dimension 0, may hold values from -6 to 6
- branch_keys: bfloat16 [8, 4096, 1024], P(('groups', 'branch'), None, 'head'), parts along dimension 0, may hold values from -6 to 6
- branch_values: bfloat16 [8, 4096, 1024], P(('groups', 'branch'), None, 'head'), parts along dimension 0, may hold values from -6 to 6
- branch_lengths: int32 [8], P(('groups', 'branch')), parts along dimension 0, may hold values from 512 to 4096, as said below
- row_branch: int32 [128], P('groups'), parts along dimension 0, may hold values from 0 to 3, as said below
Outputs:
- attended: bfloat16 [128, 8192], P(('groups', 'branch'), 'head'), parts along dimension 0
There are 2 independent parts, one for each index of `groups`. A program takes and returns all parts, laid end to end along the dimension named above; each array names one. Nothing has to cross between parts.
Inputs may be any that keep to these rules, and one draw needn't show every extreme that they name: `queries`: query entries; rows may differ in scale. `row_branch`: no branch has more than 32 rows; some branch has exactly 32. `branch_lengths`: some branch has exactly 4096 live tokens.
All inputs are finite; a program needn't handle non-finite values.
Results may differ from a plain program's by a relative error of at most 0.006.
Values may be sent and summed in bfloat16 or wider, within the bound.
A program may use at most 128 MiB of HBM per device.

v0:
```python
import functools
import math

import jax
import jax.numpy as jnp
from jax import lax
from jax.experimental import pallas as pl
from jax.experimental.pallas import tpu as pltpu
from jax.sharding import PartitionSpec as P

HD = 128
PER = 8
NEG = -1e30
MESH = pl.DeviceIdType.MESH
BF = jnp.bfloat16
F32 = jnp.float32


def split(value, parts):
    pieces = []
    for _ in range(parts):
        piece = value.astype(BF)
        pieces.append(piece)
        value = value - piece.astype(F32)
    return pieces


def kernel(
    n, rows, tokens, groups, tb,
    q_ref, rb_ref, len_ref, rk_ref, rv_ref, bk_ref, bv_ref, out_ref,
    qall, kbuf, vbuf, sbuf, mbuf, acc, rnum, rm, right, spread_e,
    send_o, send_l, recv_o, recv_l,
    kv_sem, q_own, q_send, q_recv, o_send, o_recv, l_send, l_recv,
):
    me = lax.axis_index("branch")
    slots = 2 * rows
    m_rows = slots * PER
    chunks = n // 2
    all_rows = n * rows
    part = rows * PER
    blocks = tokens // tb
    factor = math.log2(math.e) / math.sqrt(HD)

    copies = [
        pltpu.make_async_copy(src, dst, kv_sem.at[i])
        for i, (src, dst) in enumerate((
            (rk_ref, kbuf.at[0]), (rv_ref, vbuf.at[0]),
            (bk_ref.at[0], kbuf.at[1]), (bv_ref.at[0], vbuf.at[1]),
        ))
    ]
    own = pltpu.make_async_copy(q_ref, qall.at[me], q_own)
    own.start()
    copies[2].start()

    barrier = pltpu.get_barrier_semaphore()
    for off in range(1, n):
        peer = me ^ off
        pl.semaphore_signal(barrier, inc=1, device_id={"branch": peer}, device_id_type=MESH)
    pl.semaphore_wait(barrier, n - 1)

    q_copies = {}
    for g in range(groups):
        for off in reversed(range(1, n)):
            peer = me ^ off
            cols = pl.ds(g * PER * HD, PER * HD)
            copy = pltpu.make_async_remote_copy(
                src_ref=q_ref.at[:, cols], dst_ref=qall.at[me, :, cols],
                send_sem=q_send.at[g, off], recv_sem=q_recv.at[g, off],
                device_id={"branch": peer}, device_id_type=MESH,
            )
            copy.start()
            q_copies[g, off] = copy
    copies[3].start()

    rb = rb_ref[...]
    mem_row = jnp.where(rb == me, 1.0, 0.0).astype(F32)
    r_sub = lax.broadcasted_iota(jnp.int32, (all_rows, all_rows), 0)
    r_lane = lax.broadcasted_iota(jnp.int32, (all_rows, all_rows), 1)
    mem_b = jnp.broadcast_to(mem_row, (all_rows, all_rows))
    mem_col = jnp.sum(jnp.where(r_sub == r_lane, mem_b, 0.0), axis=1, keepdims=True)
    rank_col = jnp.sum(jnp.where(r_lane < r_sub, mem_b, 0.0), axis=1, keepdims=True)
    mem_cb = jnp.broadcast_to(mem_col, (all_rows, all_rows))
    rank_row = jnp.sum(jnp.where(r_sub < r_lane, mem_cb, 0.0), axis=0, keepdims=True)
    slot_sub = lax.broadcasted_iota(jnp.int32, (slots, all_rows), 0).astype(F32)
    picker = jnp.where(
        (jnp.broadcast_to(rank_row, (slots, all_rows)) == slot_sub)
        & (jnp.broadcast_to(mem_row, (slots, all_rows)) > 0.5), 1.0, 0.0,
    ).astype(BF)
    slot_lane = lax.broadcasted_iota(jnp.int32, (all_rows, slots), 1).astype(F32)
    e_full = jnp.where(
        (jnp.broadcast_to(rank_col, (all_rows, slots)) == slot_lane)
        & (jnp.broadcast_to(mem_col, (all_rows, slots)) > 0.5), 1.0, 0.0,
    ).astype(BF)
    spread_e[...] = e_full
    length = len_ref[0]

    def stack(q):
        return jnp.concatenate([q[:, p * HD:(p + 1) * HD] for p in range(PER)], axis=0)

    tasks = []
    for g in range(groups):
        tasks += [(1, g, 0)] + [(0, g, k) for k in range(1, chunks)]
    tasks += [(0, g, 0) for g in range(groups)]

    waited = set()
    started = {2, 3}

    def need(index):
        if index not in waited:
            waited.add(index)
            copies[index].wait()

    def launch(index):
        if index not in started:
            started.add(index)
            copies[index].start()

    def need_q(g, off):
        key = ("q", g, off)
        if key not in waited:
            waited.add(key)
            if off > 0:
                q_copies[g, off].wait_recv()
            elif ("own",) not in waited:
                waited.add(("own",))
                own.wait()

    def stage(first, second, slot):
        if first is not None:
            src, g, k = first
            cols = slice(g * PER * HD, (g + 1) * PER * HD)
            launch(2 * src)
            need(2 * src)
            launch(2 * src + 1)
            launch(0)
            if second is not None:
                launch(1)
            if src == 0:
                need_q(g, 2 * k)
                need_q(g, 2 * k + 1)
                base = (me // 2) ^ k
                query = stack(qall[pl.ds(base * 2, 2), :, cols].reshape(slots, PER * HD))
            else:
                for off in range(n):
                    need_q(g, off)
                whole = qall[:, :, cols].reshape(all_rows, PER * HD)
                query = stack(jnp.dot(picker, whole, preferred_element_type=F32).astype(BF))
            mbuf[slot] = jnp.full((m_rows, HD), NEG, F32)
        if second is not None:
            src2, g2, k2 = second
            need(2 * src2 + 1)
            other = 1 - slot
            peak = jnp.max(mbuf[other], axis=1, keepdims=True) * factor
            mbuf[other] = jnp.broadcast_to(peak, (m_rows, HD))
            acc[...] = jnp.zeros_like(acc)

        def body(j, carry):
            start = pl.multiple_of(j * tb, tb)
            if first is not None:
                keys = kbuf[src, pl.ds(start, tb), g * HD:(g + 1) * HD]
                score = lax.dot_general(
                    query, keys, (((1,), (1,)), ((), ())), preferred_element_type=F32
                )
                if src == 1:
                    place = start + lax.broadcasted_iota(jnp.int32, (m_rows, tb), 1)
                    score = jnp.where(place < length, score, NEG)
                top = score[:, :HD]
                for i in range(1, tb // HD):
                    top = jnp.maximum(top, score[:, i * HD:(i + 1) * HD])
                sbuf[slot, j] = score
                mbuf[slot] = jnp.maximum(mbuf[slot], top)
            if second is not None:
                top2 = mbuf[other]
                peaks = jnp.concatenate([top2] * (tb // HD), axis=1)
                weights = jnp.exp2(sbuf[other, j] * factor - peaks).astype(BF)
                values = vbuf[src2, pl.ds(start, tb), g2 * HD:(g2 + 1) * HD]
                wide = jnp.concatenate([values, jnp.ones((tb, HD), BF)], axis=1)
                acc[...] += jnp.dot(weights, wide, preferred_element_type=F32)
            return carry

        lax.fori_loop(0, blocks, body, 0)

        if second is not None and src2 == 0:
            rnum[g2, k2] = acc[...]
            rm[g2, k2] = mbuf[other]
        elif second is not None:
            numer, total, top = acc[:, :HD], acc[:, HD:], mbuf[other]
            for p in range(PER):
                lo, hi = p * slots, (p + 1) * slots
                gap = [jnp.zeros((slots, HD), BF)]
                pieces = (split(numer[lo:hi], 2) + gap, split(total[lo:hi], 2) + gap, split(top[lo:hi], 3))
                right[g2, p] = jnp.concatenate(
                    [jnp.concatenate(piece, axis=0) for piece in pieces], axis=1
                )

    eye = (
        lax.broadcasted_iota(jnp.int32, (part, part), 0)
        == lax.broadcasted_iota(jnp.int32, (part, part), 1)
    )
    sent = []

    def finish(g, k):
        base = (me // 2) ^ k
        e = spread_e[pl.ds(pl.multiple_of(base * slots, slots), slots), :]
        e3 = jnp.concatenate([e, e, e], axis=1)
        has = jnp.sum(e.astype(F32), axis=1, keepdims=True) > 0.5
        has = jnp.broadcast_to(has, (slots, HD))
        whole_o, whole_l = [], []
        for p in range(PER):
            lo, hi = p * slots, (p + 1) * slots
            back = jnp.dot(e3, right[g, p], preferred_element_type=F32)
            r_num = rnum[g, k, lo:hi, :HD]
            r_tot = rnum[g, k, lo:hi, HD:]
            r_top = rm[g, k, lo:hi]
            b_top = jnp.where(has, back[:, 2 * HD:], NEG)
            peak = jnp.maximum(r_top, b_top)
            x = jnp.exp2(r_top - peak)
            y = jnp.exp2(b_top - peak)
            num = r_num * x + back[:, :HD] * y
            tot = r_tot * x + back[:, HD:2 * HD] * y
            whole_o.append((num / tot).astype(BF))
            whole_l.append(peak + jnp.log2(tot))
        for half in range(2):
            off_slot = 2 * k + half
            lo, hi = half * rows, (half + 1) * rows
            send_o[g, off_slot] = jnp.concatenate([o[lo:hi] for o in whole_o], axis=0)
            lse = jnp.concatenate([v[lo:hi] for v in whole_l], axis=0)
            line = jnp.sum(jnp.where(eye, lse, 0.0), axis=0, keepdims=True)
            send_l[g, off_slot] = jnp.broadcast_to(line, (8, part))
        for off in range(max(1, 2 * k), 2 * k + 2):
            peer = me ^ off
            index = 2 * k + lax.rem(peer, 2)
            pair = []
            for src, dst, s_sem, r_sem in (
                (send_o, recv_o, o_send, o_recv), (send_l, recv_l, l_send, l_recv),
            ):
                copy = pltpu.make_async_remote_copy(
                    src_ref=src.at[g, index], dst_ref=dst.at[g, off],
                    send_sem=s_sem.at[g, off], recv_sem=r_sem.at[g, off],
                    device_id={"branch": peer}, device_id_type=MESH,
                )
                copy.start()
                pair.append(copy)
            sent.append((g, off, pair))

    def collect(g):
        mine = lax.rem(me, 2)
        lines = [send_l[g, mine][:1]]
        outs = [send_o[g, mine]]
        for gg, off, pair in sent:
            if gg == g:
                for copy in pair:
                    copy.wait_recv()
                lines.append(recv_l[g, off][:1])
                outs.append(recv_o[g, off])
        peak = functools.reduce(jnp.maximum, lines)
        scales = [jnp.exp2(line - peak) for line in lines]
        inverse = 1.0 / functools.reduce(jnp.add, scales)
        result = jnp.zeros((part, HD), F32)
        for scale, o in zip(scales, outs):
            diag = jnp.where(eye, jnp.broadcast_to(scale * inverse, (part, part)), 0.0)
            left = jnp.concatenate(split(diag, 2), axis=1)
            result += jnp.dot(left, jnp.concatenate([o, o], axis=0), preferred_element_type=F32)
        result = result.astype(BF)
        for p in range(PER):
            out_ref[:, (g * PER + p) * HD:(g * PER + p + 1) * HD] = result[p * rows:(p + 1) * rows]

    previous = None
    done, finished = set(), set()
    for t, task in enumerate(tasks + [None]):
        stage(task, previous, t % 2)
        if previous is not None:
            done.add(previous)
            for g in range(groups):
                for k in reversed(range(chunks)):
                    if (1, g, 0) in done and (0, g, k) in done and (g, k) not in finished:
                        finished.add((g, k))
                        finish(g, k)
        previous = task
    for g in range(groups):
        collect(g)
    for copy in q_copies.values():
        copy.wait_send()
    for _, _, pair in sent:
        for copy in pair:
            copy.wait_send()


def on_device(
    queries, root_keys, root_values, branch_keys, branch_values, branch_lengths, row_branch
):
    rows = queries.shape[0]
    all_rows = row_branch.shape[0]
    n = all_rows // rows
    tokens, width = root_keys.shape
    groups = width // HD
    chunks = n // 2
    slots = 2 * rows
    m_rows = slots * PER
    part = rows * PER
    tb = min(2048, tokens)
    vmem = pl.BlockSpec(memory_space=pltpu.VMEM)
    smem = pl.BlockSpec(memory_space=pltpu.SMEM)
    hbm = pl.BlockSpec(memory_space=pl.ANY)
    dma = pltpu.SemaphoreType.DMA
    return pl.pallas_call(
        functools.partial(kernel, n, rows, tokens, groups, tb),
        out_shape=jax.ShapeDtypeStruct(queries.shape, BF),
        in_specs=[vmem, vmem, smem, hbm, hbm, hbm, hbm],
        out_specs=vmem,
        scratch_shapes=[
            pltpu.VMEM((n, rows, groups * PER * HD), BF),
            pltpu.VMEM((2, tokens, width), BF),
            pltpu.VMEM((2, tokens, width), BF),
            pltpu.VMEM((2, tokens // tb, m_rows, tb), F32),
            pltpu.VMEM((2, m_rows, HD), F32),
            pltpu.VMEM((m_rows, 2 * HD), F32),
            pltpu.VMEM((groups, chunks, m_rows, 2 * HD), F32),
            pltpu.VMEM((groups, chunks, m_rows, HD), F32),
            pltpu.VMEM((groups, PER, 3 * slots, 3 * HD), BF),
            pltpu.VMEM((all_rows, slots), BF),
            pltpu.VMEM((groups, n, part, HD), BF),
            pltpu.VMEM((groups, n, 8, part), F32),
            pltpu.VMEM((groups, n, part, HD), BF),
            pltpu.VMEM((groups, n, 8, part), F32),
            dma((4,)), dma, dma((groups, n)), dma((groups, n)),
            dma((groups, n)), dma((groups, n)), dma((groups, n)), dma((groups, n)),
        ],
        compiler_params=pltpu.CompilerParams(
            collective_id=0, has_side_effects=True, vmem_limit_bytes=60 * 1024 * 1024
        ),
        name="cascade",
    )(queries, row_branch.reshape(1, all_rows), branch_lengths, root_keys, root_values, branch_keys, branch_values)


def solution(mesh):
    placed = (
        P(("groups", "branch"), "head"),
        P(("groups", "branch"), "head"),
        P(("groups", "branch"), "head"),
        P(("groups", "branch"), None, "head"),
        P(("groups", "branch"), None, "head"),
        P(("groups", "branch")),
        P("groups"),
    )
    return jax.shard_map(
        on_device,
        mesh=mesh,
        in_specs=placed,
        out_specs=P(("groups", "branch"), "head"),
        check_vma=False,
    )
```

profile of v0, /device:TPU:0, one launch (start us, length us, event | category | flops | bytes accessed | tf_op | source)
XLA Modules:
  0.0 22.5 jit_solution(15700531777459688362)
XLA Ops:
  0.7 20.3 %cascade.1 = bf16[16,2048]{1,0:T(8,128)(2,1)} custom-call(bf16[16,2048]{1,0:T(8,128)(2,1)} %q_ref.1, s32[1,64]{1,0:T(1,128)} %bitcast.1, s32[1]{0:T(128)S(6)} %copy.9.len_ref, bf16[4096,256]{1,0:T(8,128)(2,1)} %rk_ref.1, bf16[4096,256]{1,0:T(8,128)(2,1)} %rv_ref.1, bf16[1,4096,256]{2,1,0:T(8,128)(2,1)} %bk_ref.1, bf16[1,4096,256]{2,1,0:T(8,128)(2,1)} %bv_ref.1), custom_call_target="tpu_custom_call" | custom-call | tf_op jit(solution)/shard_map/cascade/pallas_call | solution.py:306
  21.0 1.5 %copy.10 = bf16[16,2048]{1,0:T(8,128)(2,1)} copy(bf16[16,2048]{1,0:T(8,128)(2,1)} %cascade.1) | data formatting | bytes 131072
where the time goes:
time: 22.7 us; the launch traced here: 22.5 us
  Pallas kernels  20.3 us (89%)
  local copies, waits for them, and re-layouts  1.47 us (6%)
  between operations  0.66 us (3%)
    pallas_call x1, Pallas kernels, on_device(): pl.pallas_call(functools.partial(kernel, n, rows, tokens, groups, tb), ou...  20.3 us
    unnamed x1, local copies, waits for them, and re-layouts  1.47 us

commit v1 on v0

v1 whole, which is shorter than its diff:
```python
import functools
import math

import jax
import jax.numpy as jnp
from jax import lax
from jax.experimental import pallas as pl
from jax.experimental.pallas import tpu as pltpu
from jax.sharding import PartitionSpec as P

HD = 128
PER = 8
NEG = -1e30
STAT = 16
MESH = pl.DeviceIdType.MESH
BF = jnp.bfloat16
F32 = jnp.float32
SPLIT_DIMS = (((1,), (1,)), ((), ()))


def split(value, parts):
    pieces = []
    for _ in range(parts):
        piece = value.astype(BF)
        pieces.append(piece)
        value = value - piece.astype(F32)
    return pieces


def kernel(
    n, rows, tokens, groups, tb,
    q_ref, rb_ref, len_ref, rk_ref, rv_ref, bk_ref, bv_ref, out_ref,
    qall, kbuf, vbuf, vt, sbuf0, sbuf1, mbuf0, mbuf1, rnum, rm, right, place_e, rbuf, lbuf,
    send, recv,
    kv_sem, small_sem, q_send, q_recv, o_send, o_recv,
):
    me = lax.axis_index("branch")
    slots = 2 * rows
    cols = slots * PER
    part = rows * PER
    chunks = n // 2
    all_rows = n * rows
    sbufs, mbufs = (sbuf0, sbuf1), (mbuf0, mbuf1)
    factor = math.log2(math.e) / math.sqrt(HD)

    copies = [
        pltpu.make_async_copy(src, dst, kv_sem.at[i])
        for i, (src, dst) in enumerate((
            (rk_ref, kbuf.at[0]), (rv_ref, vbuf.at[0]),
            (bk_ref.at[0], kbuf.at[1]), (bv_ref.at[0], vbuf.at[1]),
        ))
    ]
    own = pltpu.make_async_copy(q_ref, qall.at[me], small_sem.at[0])
    rb_copy = pltpu.make_async_copy(rb_ref, rbuf, small_sem.at[1])
    len_copy = pltpu.make_async_copy(len_ref, lbuf, small_sem.at[2])
    own.start()
    rb_copy.start()
    len_copy.start()
    copies[0].start()

    barrier = pltpu.get_barrier_semaphore()
    for off in range(1, n):
        peer = me ^ off
        pl.semaphore_signal(barrier, inc=1, device_id={"branch": peer}, device_id_type=MESH)
    copies[1].start()
    rb_copy.wait()
    len_copy.wait()
    rb = rbuf[...]
    mem_row = jnp.where(rb == me, 1.0, 0.0).astype(F32)
    r_sub = lax.broadcasted_iota(jnp.int32, (all_rows, all_rows), 0)
    r_lane = lax.broadcasted_iota(jnp.int32, (all_rows, all_rows), 1)
    mem_b = jnp.broadcast_to(mem_row, (all_rows, all_rows))
    mem_col = jnp.sum(jnp.where(r_sub == r_lane, mem_b, 0.0), axis=1, keepdims=True)
    mem_cb = jnp.broadcast_to(mem_col, (all_rows, all_rows))
    rank_row = jnp.sum(jnp.where(r_sub < r_lane, mem_cb, 0.0), axis=0, keepdims=True)
    slot_sub = lax.broadcasted_iota(jnp.int32, (slots, all_rows), 0).astype(F32)
    picker = jnp.where(
        (jnp.broadcast_to(rank_row, (slots, all_rows)) == slot_sub)
        & (jnp.broadcast_to(mem_row, (slots, all_rows)) > 0.5), 1.0, 0.0,
    ).astype(BF)
    sub = lax.broadcasted_iota(jnp.int32, (cols, part), 0)
    lane = lax.broadcasted_iota(jnp.int32, (cols, part), 1)
    same = (sub // slots) == (lane // rows)
    t_sub = lax.broadcasted_iota(jnp.int32, (all_rows, part), 0)
    t_lane = lax.broadcasted_iota(jnp.int32, (all_rows, part), 1)
    for d in range(n):
        spread = jnp.where(t_sub == d * rows + lax.rem(t_lane, rows), 1.0, 0.0).astype(BF)
        wide = jnp.dot(picker, spread, preferred_element_type=F32)
        wide = jnp.concatenate([wide] * PER, axis=0)
        place_e[d] = jnp.where(same, wide, 0.0).astype(BF)
    length = jnp.full((8, cols), lbuf[0], jnp.int32)

    own.wait()
    pl.semaphore_wait(barrier, n - 1)

    q_copies = {}
    for g in range(groups):
        for off in range(1, n):
            peer = me ^ off
            lanes = pl.ds(g * PER * HD, PER * HD)
            copy = pltpu.make_async_remote_copy(
                src_ref=qall.at[me, :, lanes], dst_ref=qall.at[me, :, lanes],
                send_sem=q_send.at[g, off], recv_sem=q_recv.at[g, off],
                device_id={"branch": peer}, device_id_type=MESH,
            )
            copy.start()
            q_copies[g, off] = copy
    copies[2].start()
    copies[3].start()

    def stack(q):
        return jnp.concatenate([q[:, p * HD:(p + 1) * HD] for p in range(PER)], axis=0)

    tasks = [(0, g, 0) for g in range(groups)]
    for g in range(groups):
        tasks += [(1, g, 0)] + [(0, g, k) for k in range(1, chunks)]

    waited = set()

    def once(key, fn):
        if key not in waited:
            waited.add(key)
            fn()

    def need_q(g, off):
        if off > 0:
            once(("q", g, off), q_copies[g, off].wait_recv)

    def stage(first, second, slot):
        other = 1 - slot
        if first is not None:
            src, g, k = first
            lanes = slice(g * PER * HD, (g + 1) * PER * HD)
            once(2 * src, copies[2 * src].wait)
            if src == 0:
                need_q(g, 2 * k)
                need_q(g, 2 * k + 1)
                base = (me // 2) ^ k
                query = jnp.concatenate(
                    [stack(qall[base * 2 + i, :, lanes]) for i in range(2)], axis=0
                )
            else:
                for off in range(n):
                    need_q(g, off)
                whole = qall[:, :, lanes].reshape(all_rows, PER * HD)
                query = stack(jnp.dot(picker, whole, preferred_element_type=F32).astype(BF))
        run = jnp.full((8, cols), NEG, F32)
        total = jnp.zeros((HD + STAT, cols), F32)
        if second is not None:
            src2, g2, k2 = second
            once(2 * src2 + 1, copies[2 * src2 + 1].wait)
            peak = jnp.max(mbufs[other][...], axis=0, keepdims=True) * factor
            top = jnp.broadcast_to(peak, (8, cols))
            fresh = ("vt", src2, g2) not in waited

        for start in range(0, tokens, tb):
            tile = slice(start, start + tb)
            if first is not None:
                keys = kbuf[src, tile, g * HD:(g + 1) * HD]
                score = lax.dot_general(keys, query, SPLIT_DIMS, preferred_element_type=F32)
                score = score.reshape(tb // 8, 8, cols)
                if src == 1:
                    place = start + 8 * lax.broadcasted_iota(jnp.int32, (tb // 8, 8, cols), 0)
                    place = place + lax.broadcasted_iota(jnp.int32, (tb // 8, 8, cols), 1)
                    score = jnp.where(place < length[None], score, NEG)
                run = jnp.maximum(run, jnp.max(score, axis=0))
                sbufs[slot][tile] = score.reshape(tb, cols)
            if second is not None:
                s2 = sbufs[other][tile].reshape(tb // 8, 8, cols)
                weights = jnp.exp2(s2 * factor - top[None]).reshape(tb, cols).astype(BF)
                if fresh:
                    v = jnp.transpose(vbuf[src2, tile, g2 * HD:(g2 + 1) * HD])
                    if src2 == 0 and chunks > 1:
                        vt[g2, :, tile] = v
                else:
                    v = vt[g2, :, tile]
                left = jnp.concatenate([v, jnp.ones((STAT, tb), BF)], axis=0)
                total = total + jnp.dot(left, weights, preferred_element_type=F32)

        if first is not None:
            mbufs[slot][...] = run
        if second is not None:
            waited.add(("vt", src2, g2))
            if src2 == 0:
                rnum[g2, k2] = total
                rm[g2, k2] = top
            else:
                hi, lo = split(total[:HD], 2)
                stats = split(total[HD:HD + 1], 2) + split(peak, 3)
                stats += [jnp.zeros((1, cols), BF)] * (STAT - 5)
                right[g2] = jnp.concatenate([hi, lo] + stats, axis=0)

    sent = []

    def finish(g, k):
        base = (me // 2) ^ k
        e = jnp.concatenate([place_e[base * 2], place_e[base * 2 + 1]], axis=1)
        has = jnp.sum(e.astype(F32), axis=0, keepdims=True) > 0.5
        back = jnp.dot(right[g], e, preferred_element_type=F32)
        b_num = back[:HD] + back[HD:2 * HD]
        b_tot = back[2 * HD:2 * HD + 1] + back[2 * HD + 1:2 * HD + 2]
        b_top = back[2 * HD + 2:2 * HD + 3] + back[2 * HD + 3:2 * HD + 4] + back[2 * HD + 4:2 * HD + 5]
        b_top = jnp.where(has, b_top, NEG)
        r_num = rnum[g, k, :HD]
        r_tot = rnum[g, k, HD:HD + 1]
        r_top = rm[g, k, :1]
        peak = jnp.maximum(r_top, b_top)
        x = jnp.exp2(r_top - peak)
        y = jnp.exp2(b_top - peak)
        tot = r_tot * x + b_tot * y
        inverse = 1.0 / tot
        out = (r_num * (x * inverse) + b_num * (y * inverse)).astype(BF)
        lse = split(peak + jnp.log2(tot), 3)
        lse = jnp.concatenate(lse + [jnp.zeros((1, cols), BF)] * (STAT - 3), axis=0)
        for half in range(2):
            lo, hi = half * part, (half + 1) * part
            send[g, 2 * k + half, :HD] = out[:, lo:hi]
            send[g, 2 * k + half, HD:] = lse[:, lo:hi]
        for off in range(max(1, 2 * k), 2 * k + 2):
            peer = me ^ off
            index = 2 * k + lax.rem(peer, 2)
            copy = pltpu.make_async_remote_copy(
                src_ref=send.at[g, index], dst_ref=recv.at[g, off],
                send_sem=o_send.at[g, off], recv_sem=o_recv.at[g, off],
                device_id={"branch": peer}, device_id_type=MESH,
            )
            copy.start()
            sent.append((g, off, copy))

    def collect(g):
        blocks_in = [send[g, lax.rem(me, 2)]]
        for gg, off, copy in sent:
            if gg == g:
                copy.wait_recv()
                blocks_in.append(recv[g, off])
        lses, outs = [], []
        for block in blocks_in:
            stat = block[HD:].astype(F32)
            lses.append(stat[0:1] + stat[1:2] + stat[2:3])
            outs.append(block[:HD].astype(F32))
        peak = functools.reduce(jnp.maximum, lses)
        scales = [jnp.exp2(line - peak) for line in lses]
        inverse = 1.0 / functools.reduce(jnp.add, scales)
        result = functools.reduce(
            jnp.add, [o * (scale * inverse) for o, scale in zip(outs, scales)]
        )
        result = jnp.transpose(result).astype(BF)
        for p in range(PER):
            out_ref[:, (g * PER + p) * HD:(g * PER + p + 1) * HD] = result[p * rows:(p + 1) * rows]

    previous = None
    done, finished = set(), set()
    for t, task in enumerate(tasks + [None]):
        stage(task, previous, t % 2)
        if previous is not None:
            done.add(previous)
            for g in range(groups):
                for k in reversed(range(chunks)):
                    if (1, g, 0) in done and (0, g, k) in done and (g, k) not in finished:
                        finished.add((g, k))
                        finish(g, k)
        previous = task
    for g in range(groups):
        collect(g)
    for copy in q_copies.values():
        copy.wait_send()
    for _, _, copy in sent:
        copy.wait_send()


def on_device(
    queries, root_keys, root_values, branch_keys, branch_values, branch_lengths, row_branch
):
    rows = queries.shape[0]
    all_rows = row_branch.shape[0]
    n = all_rows // rows
    tokens, width = root_keys.shape
    groups = width // HD
    chunks = n // 2
    slots = 2 * rows
    cols = slots * PER
    part = rows * PER
    tb = min(TB, tokens)
    vmem = pl.BlockSpec(memory_space=pltpu.VMEM)
    hbm = pl.BlockSpec(memory_space=pl.ANY)
    dma = pltpu.SemaphoreType.DMA
    return pl.pallas_call(
        functools.partial(kernel, n, rows, tokens, groups, tb),
        out_shape=pltpu.VMEM(queries.shape, BF),
        in_specs=[hbm] * 7,
        out_specs=vmem,
        scratch_shapes=[
            pltpu.VMEM((n, rows, groups * PER * HD), BF),
            pltpu.VMEM((2, tokens, width), BF),
            pltpu.VMEM((2, tokens, width), BF),
            pltpu.VMEM((groups, HD, tokens), BF),
            pltpu.VMEM((tokens, cols), F32),
            pltpu.VMEM((tokens, cols), F32),
            pltpu.VMEM((8, cols), F32),
            pltpu.VMEM((8, cols), F32),
            pltpu.VMEM((groups, chunks, HD + STAT, cols), F32),
            pltpu.VMEM((groups, chunks, 8, cols), F32),
            pltpu.VMEM((groups, 2 * HD + STAT, cols), BF),
            pltpu.VMEM((n, cols, part), BF),
            pltpu.VMEM((1, all_rows), jnp.int32),
            pltpu.SMEM((1,), jnp.int32),
            pltpu.VMEM((groups, n, HD + STAT, part), BF),
            pltpu.VMEM((groups, n, HD + STAT, part), BF),
            dma((4,)), dma((3,)), dma((groups, n)), dma((groups, n)),
            dma((groups, n)), dma((groups, n)),
        ],
        compiler_params=pltpu.CompilerParams(
            collective_id=0, has_side_effects=True, vmem_limit_bytes=60 * 1024 * 1024
        ),
        name="cascade",
    )(
        queries, row_branch.reshape(1, all_rows), branch_lengths,
        root_keys, root_values, branch_keys, branch_values,
    )


TB = 256


def solution(mesh):
    placed = (
        P(("groups", "branch"), "head"),
        P(("groups", "branch"), "head"),
        P(("groups", "branch"), "head"),
        P(("groups", "branch"), None, "head"),
        P(("groups", "branch"), None, "head"),
        P(("groups", "branch")),
        P("groups"),
    )
    return jax.shard_map(
        on_device,
        mesh=mesh,
        in_specs=placed,
        out_specs=P(("groups", "branch"), "head"),
        check_vma=False,
    )
```

time: 22.7 us -> 19.5 us (0.86)
  Pallas kernels: 20.3 us -> 18 us
  local copies, waits for them, and re-layouts: 1.47 us -> 0.63 us
    pallas_call x1, Pallas kernels: 20.3 us -> 18 us  [on_device(): pl.pallas_call(functools.partial(kernel, n, rows, tokens, groups, tb), ou...]
    unnamed x1, local copies, waits for them, and re-layouts: 1.47 us -> 0.63 us
where the time goes in v1:
time: 19.5 us; the launch traced here: 19.3 us
  Pallas kernels  18 us (92%)
  between operations  0.66 us (3%)
  local copies, waits for them, and re-layouts  0.63 us (3%)
    pallas_call x1, Pallas kernels, on_device(): pl.pallas_call(functools.partial(kernel, n, rows, tokens, groups, tb), ou...  18 us
    unnamed x1, local copies, waits for them, and re-layouts  0.63 us

profile of v1, /device:TPU:0, one launch (start us, length us, event | category | flops | bytes accessed | tf_op | source)
XLA Modules:
  0.0 19.3 jit_solution(7257924492560998076)
XLA Ops:
  0.7 18.0 %cascade.1 = bf16[16,2048]{1,0:T(8,128)(2,1)S(1)} custom-call(bf16[16,2048]{1,0:T(8,128)(2,1)} %q_ref.1, s32[1,64]{1,0:T(1,128)} %bitcast.1, s32[1]{0:T(128)S(6)} %copy.10.len_ref, bf16[4096,256]{1,0:T(8,128)(2,1)} %rk_ref.1, bf16[4096,256]{1,0:T(8,128)(2,1)} %rv_ref.1, bf16[1,4096,256]{2,1,0:T(8,128)(2,1)} %bk_ref.1, bf16[1,4096,256]{2,1,0:T(8,128)(2,1)} %bv_ref.1), custom_call_target="tpu_custom_call" | custom-call | tf_op jit(solution)/shard_map/cascade/pallas_call | solution.py:287
  18.7 0.6 %copy.9 = bf16[16,2048]{1,0:T(8,128)(2,1)} copy(bf16[16,2048]{1,0:T(8,128)(2,1)S(1)} %cascade.1) | data formatting | bytes 131072

commit v2 on v1

--- a/solution.py
+++ b/solution.py
@@ -12,6 +12,7 @@
 PER = 8
 NEG = -1e30
 STAT = 16
+CHAIN = 32
 MESH = pl.DeviceIdType.MESH
 BF = jnp.bfloat16
 F32 = jnp.float32
@@ -32,7 +33,7 @@
     q_ref, rb_ref, len_ref, rk_ref, rv_ref, bk_ref, bv_ref, out_ref,
     qall, kbuf, vbuf, vt, sbuf0, sbuf1, mbuf0, mbuf1, rnum, rm, right, place_e, rbuf, lbuf,
     send, recv,
-    kv_sem, small_sem, q_send, q_recv, o_send, o_recv,
+    kv_sem, small_sem, fence, q_send, q_recv, o_send, o_recv,
 ):
     me = lax.axis_index("branch")
     slots = 2 * rows
@@ -128,6 +129,8 @@
 
     def stage(first, second, slot):
         other = 1 - slot
+        pl.semaphore_signal(fence, inc=1)
+        pl.semaphore_wait(fence, 1)
         if first is not None:
             src, g, k = first
             lanes = slice(g * PER * HD, (g + 1) * PER * HD)
@@ -144,7 +147,7 @@
                     need_q(g, off)
                 whole = qall[:, :, lanes].reshape(all_rows, PER * HD)
                 query = stack(jnp.dot(picker, whole, preferred_element_type=F32).astype(BF))
-        run = jnp.full((8, cols), NEG, F32)
+        run = jnp.full((CHAIN, cols), NEG, F32)
         total = jnp.zeros((HD + STAT, cols), F32)
         if second is not None:
             src2, g2, k2 = second
@@ -163,7 +166,7 @@
                     place = start + 8 * lax.broadcasted_iota(jnp.int32, (tb // 8, 8, cols), 0)
                     place = place + lax.broadcasted_iota(jnp.int32, (tb // 8, 8, cols), 1)
                     score = jnp.where(place < length[None], score, NEG)
-                run = jnp.maximum(run, jnp.max(score, axis=0))
+                run = jnp.maximum(run, jnp.max(score.reshape(tb // CHAIN, CHAIN, cols), axis=0))
                 sbufs[slot][tile] = score.reshape(tb, cols)
             if second is not None:
                 s2 = sbufs[other][tile].reshape(tb // 8, 8, cols)
@@ -296,8 +299,8 @@
             pltpu.VMEM((groups, HD, tokens), BF),
             pltpu.VMEM((tokens, cols), F32),
             pltpu.VMEM((tokens, cols), F32),
-            pltpu.VMEM((8, cols), F32),
-            pltpu.VMEM((8, cols), F32),
+            pltpu.VMEM((CHAIN, cols), F32),
+            pltpu.VMEM((CHAIN, cols), F32),
             pltpu.VMEM((groups, chunks, HD + STAT, cols), F32),
             pltpu.VMEM((groups, chunks, 8, cols), F32),
             pltpu.VMEM((groups, 2 * HD + STAT, cols), BF),
@@ -306,7 +309,7 @@
             pltpu.SMEM((1,), jnp.int32),
             pltpu.VMEM((groups, n, HD + STAT, part), BF),
             pltpu.VMEM((groups, n, HD + STAT, part), BF),
-            dma((4,)), dma((3,)), dma((groups, n)), dma((groups, n)),
+            dma((4,)), dma((3,)), pltpu.SemaphoreType.REGULAR, dma((groups, n)), dma((groups, n)),
             dma((groups, n)), dma((groups, n)),
         ],
         compiler_params=pltpu.CompilerParams(

time: 19.5 us -> 18.8 us (0.964)
  Pallas kernels: 18 us -> 17.4 us
    pallas_call x1, Pallas kernels: 18 us -> 17.4 us  [on_device(): pl.pallas_call(functools.partial(kernel, n, rows, tokens, groups, tb), ou...]
where the time goes in v2:
time: 18.8 us; the launch traced here: 18.7 us
  Pallas kernels  17.4 us (93%)
  between operations  0.66 us (4%)
  local copies, waits for them, and re-layouts  0.63 us (3%)
    pallas_call x1, Pallas kernels, on_device(): pl.pallas_call(functools.partial(kernel, n, rows, tokens, groups, tb), ou...  17.4 us
    unnamed x1, local copies, waits for them, and re-layouts  0.63 us

profile of v2, /device:TPU:0, one launch (start us, length us, event | category | flops | bytes accessed | tf_op | source)
XLA Modules:
  0.0 18.7 jit_solution(1745900936579803762)
XLA Ops:
  0.7 17.4 %cascade.1 = bf16[16,2048]{1,0:T(8,128)(2,1)S(1)} custom-call(bf16[16,2048]{1,0:T(8,128)(2,1)} %q_ref.1, s32[1,64]{1,0:T(1,128)} %bitcast.1, s32[1]{0:T(128)S(6)} %copy.10.len_ref, bf16[4096,256]{1,0:T(8,128)(2,1)} %rk_ref.1, bf16[4096,256]{1,0:T(8,128)(2,1)} %rv_ref.1, bf16[1,4096,256]{2,1,0:T(8,128)(2,1)} %bk_ref.1, bf16[1,4096,256]{2,1,0:T(8,128)(2,1)} %bv_ref.1), custom_call_target="tpu_custom_call" | custom-call | tf_op jit(solution)/shard_map/cascade/pallas_call | solution.py:290
  18.1 0.6 %copy.9 = bf16[16,2048]{1,0:T(8,128)(2,1)} copy(bf16[16,2048]{1,0:T(8,128)(2,1)S(1)} %cascade.1) | data formatting | bytes 131072

commit v3 on v2

--- a/solution.py
+++ b/solution.py
@@ -31,7 +31,7 @@
 def kernel(
     n, rows, tokens, groups, tb,
     q_ref, rb_ref, len_ref, rk_ref, rv_ref, bk_ref, bv_ref, out_ref,
-    qall, kbuf, vbuf, vt, sbuf0, sbuf1, mbuf0, mbuf1, rnum, rm, right, place_e, rbuf, lbuf,
+    qall, qcur, kbuf, vbuf, sbuf, mbuf, pnum, ptop, right, place_e, rbuf, lbuf,
     send, recv,
     kv_sem, small_sem, fence, q_send, q_recv, o_send, o_recv,
 ):
@@ -41,7 +41,6 @@
     part = rows * PER
     chunks = n // 2
     all_rows = n * rows
-    sbufs, mbufs = (sbuf0, sbuf1), (mbuf0, mbuf1)
     factor = math.log2(math.e) / math.sqrt(HD)
 
     copies = [
@@ -63,7 +62,8 @@
     for off in range(1, n):
         peer = me ^ off
         pl.semaphore_signal(barrier, inc=1, device_id={"branch": peer}, device_id_type=MESH)
-    copies[1].start()
+    for copy in copies[1:]:
+        copy.start()
     rb_copy.wait()
     len_copy.wait()
     rb = rbuf[...]
@@ -106,8 +106,6 @@
             )
             copy.start()
             q_copies[g, off] = copy
-    copies[2].start()
-    copies[3].start()
 
     def stack(q):
         return jnp.concatenate([q[:, p * HD:(p + 1) * HD] for p in range(PER)], axis=0)
@@ -115,85 +113,102 @@
     tasks = [(0, g, 0) for g in range(groups)]
     for g in range(groups):
         tasks += [(1, g, 0)] + [(0, g, k) for k in range(1, chunks)]
+    place_of = {task: t for t, task in enumerate(tasks)}
+    last = len(tasks)
 
     waited = set()
 
-    def once(key, fn):
-        if key not in waited:
-            waited.add(key)
-            fn()
-
     def need_q(g, off):
-        if off > 0:
-            once(("q", g, off), q_copies[g, off].wait_recv)
-
-    def stage(first, second, slot):
-        other = 1 - slot
+        if off > 0 and (g, off) not in waited:
+            waited.add((g, off))
+            q_copies[g, off].wait_recv()
+
+    def load_query(t):
+        src, g, k = tasks[t]
+        lanes = slice(g * PER * HD, (g + 1) * PER * HD)
+        if src == 0:
+            need_q(g, 2 * k)
+            need_q(g, 2 * k + 1)
+            base = (me // 2) ^ k
+            for i in range(2):
+                qcur[i * part:(i + 1) * part] = stack(qall[base * 2 + i, :, lanes])
+        else:
+            if t == groups:
+                copies[2].wait()
+                copies[3].wait()
+            for off in range(n):
+                need_q(g, off)
+            whole = qall[:, :, lanes].reshape(all_rows, PER * HD)
+            qcur[...] = stack(jnp.dot(picker, whole, preferred_element_type=F32).astype(BF))
+
+    def fence_here():
         pl.semaphore_signal(fence, inc=1)
         pl.semaphore_wait(fence, 1)
-        if first is not None:
-            src, g, k = first
-            lanes = slice(g * PER * HD, (g + 1) * PER * HD)
-            once(2 * src, copies[2 * src].wait)
-            if src == 0:
-                need_q(g, 2 * k)
-                need_q(g, 2 * k + 1)
-                base = (me // 2) ^ k
-                query = jnp.concatenate(
-                    [stack(qall[base * 2 + i, :, lanes]) for i in range(2)], axis=0
-                )
-            else:
-                for off in range(n):
-                    need_q(g, off)
-                whole = qall[:, :, lanes].reshape(all_rows, PER * HD)
-                query = stack(jnp.dot(picker, whole, preferred_element_type=F32).astype(BF))
+
+    def buffer_of(t):
+        late = t - groups
+        step = lax.rem(late, chunks)
+        first = jnp.where(step == 0, groups + late // chunks, late // chunks)
+        return jnp.where(t < groups, t, first)
+
+    def lanes_of(at):
+        return pl.ds(pl.multiple_of(lax.rem(at, groups) * HD, HD), HD)
+
+    def stage(t, first, second, masked):
+        if first:
+            at = buffer_of(t) if masked else jnp.int32(t)
+            query = qcur[...]
+            limit = jnp.where(at >= groups, length, tokens) if masked else None
+        if second:
+            at2 = buffer_of(t - 1) if masked else buffer_of(jnp.int32(t - 1))
+            peak = jnp.max(mbuf[...], axis=0, keepdims=True) * factor
+            top = jnp.broadcast_to(peak, (8, cols))
         run = jnp.full((CHAIN, cols), NEG, F32)
         total = jnp.zeros((HD + STAT, cols), F32)
-        if second is not None:
-            src2, g2, k2 = second
-            once(2 * src2 + 1, copies[2 * src2 + 1].wait)
-            peak = jnp.max(mbufs[other][...], axis=0, keepdims=True) * factor
-            top = jnp.broadcast_to(peak, (8, cols))
-            fresh = ("vt", src2, g2) not in waited
-
         for start in range(0, tokens, tb):
             tile = slice(start, start + tb)
-            if first is not None:
-                keys = kbuf[src, tile, g * HD:(g + 1) * HD]
-                score = lax.dot_general(keys, query, SPLIT_DIMS, preferred_element_type=F32)
-                score = score.reshape(tb // 8, 8, cols)
-                if src == 1:
+            if second:
+                s2 = sbuf[tile].reshape(tb // 8, 8, cols)
+                weights = jnp.exp2(s2 * factor - top[None]).reshape(tb, cols).astype(BF)
+            if first:
+                score = lax.dot_general(kbuf[at // groups, tile, lanes_of(at)], query, SPLIT_DIMS, preferred_element_type=F32)
+                if masked:
+                    score = score.reshape(tb // 8, 8, cols)
                     place = start + 8 * lax.broadcasted_iota(jnp.int32, (tb // 8, 8, cols), 0)
                     place = place + lax.broadcasted_iota(jnp.int32, (tb // 8, 8, cols), 1)
-                    score = jnp.where(place < length[None], score, NEG)
-                run = jnp.maximum(run, jnp.max(score.reshape(tb // CHAIN, CHAIN, cols), axis=0))
-                sbufs[slot][tile] = score.reshape(tb, cols)
-            if second is not None:
-                s2 = sbufs[other][tile].reshape(tb // 8, 8, cols)
-                weights = jnp.exp2(s2 * factor - top[None]).reshape(tb, cols).astype(BF)
-                if fresh:
-                    v = jnp.transpose(vbuf[src2, tile, g2 * HD:(g2 + 1) * HD])
-                    if src2 == 0 and chunks > 1:
-                        vt[g2, :, tile] = v
-                else:
-                    v = vt[g2, :, tile]
+                    score = jnp.where(place < limit[None], score, NEG)
+                chains = score.reshape(tb // CHAIN, CHAIN, cols)
+                run = jnp.maximum(run, jnp.max(chains, axis=0))
+                sbuf[tile] = score.reshape(tb, cols)
+            if second:
+                v = jnp.transpose(vbuf[at2 // groups, tile, lanes_of(at2)])
                 left = jnp.concatenate([v, jnp.ones((STAT, tb), BF)], axis=0)
                 total = total + jnp.dot(left, weights, preferred_element_type=F32)
-
-        if first is not None:
-            mbufs[slot][...] = run
-        if second is not None:
-            waited.add(("vt", src2, g2))
-            if src2 == 0:
-                rnum[g2, k2] = total
-                rm[g2, k2] = top
-            else:
-                hi, lo = split(total[:HD], 2)
-                stats = split(total[HD:HD + 1], 2) + split(peak, 3)
-                stats += [jnp.zeros((1, cols), BF)] * (STAT - 5)
-                right[g2] = jnp.concatenate([hi, lo] + stats, axis=0)
+        if first:
+            mbuf[...] = run
+        if second:
+            pnum[t - 1] = total
+            ptop[t - 1] = top
 
     sent = []
+    outgoing = {}
+    for g in range(groups):
+        for off in range(1, n):
+            peer = me ^ off
+            index = 2 * (off // 2) + lax.rem(peer, 2)
+            outgoing[g, off] = pltpu.make_async_remote_copy(
+                src_ref=send.at[g, index], dst_ref=recv.at[g, off],
+                send_sem=o_send.at[g, off], recv_sem=o_recv.at[g, off],
+                device_id={"branch": peer}, device_id_type=MESH,
+            )
+            sent.append((g, off, outgoing[g, off]))
+
+    def pack_branch(g):
+        t = place_of[1, g, 0]
+        hi, lo = split(pnum[t, :HD], 2)
+        stats = split(pnum[t, HD:HD + 1], 2) + split(ptop[t, :1], 3)
+        stats += [jnp.zeros((1, cols), BF)] * (STAT - 5)
+        right[g] = jnp.concatenate([hi, lo] + stats, axis=0)
 
     def finish(g, k):
         base = (me // 2) ^ k
@@ -204,9 +219,10 @@
         b_tot = back[2 * HD:2 * HD + 1] + back[2 * HD + 1:2 * HD + 2]
         b_top = back[2 * HD + 2:2 * HD + 3] + back[2 * HD + 3:2 * HD + 4] + back[2 * HD + 4:2 * HD + 5]
         b_top = jnp.where(has, b_top, NEG)
-        r_num = rnum[g, k, :HD]
-        r_tot = rnum[g, k, HD:HD + 1]
-        r_top = rm[g, k, :1]
+        t = place_of[0, g, k]
+        r_num = pnum[t, :HD]
+        r_tot = pnum[t, HD:HD + 1]
+        r_top = ptop[t, :1]
         peak = jnp.maximum(r_top, b_top)
         x = jnp.exp2(r_top - peak)
         y = jnp.exp2(b_top - peak)
@@ -220,15 +236,7 @@
             send[g, 2 * k + half, :HD] = out[:, lo:hi]
             send[g, 2 * k + half, HD:] = lse[:, lo:hi]
         for off in range(max(1, 2 * k), 2 * k + 2):
-            peer = me ^ off
-            index = 2 * k + lax.rem(peer, 2)
-            copy = pltpu.make_async_remote_copy(
-                src_ref=send.at[g, index], dst_ref=recv.at[g, off],
-                send_sem=o_send.at[g, off], recv_sem=o_recv.at[g, off],
-                device_id={"branch": peer}, device_id_type=MESH,
-            )
-            copy.start()
-            sent.append((g, off, copy))
+            outgoing[g, off].start()
 
     def collect(g):
         blocks_in = [send[g, lax.rem(me, 2)]]
@@ -251,18 +259,42 @@
         for p in range(PER):
             out_ref[:, (g * PER + p) * HD:(g * PER + p + 1) * HD] = result[p * rows:(p + 1) * rows]
 
-    previous = None
+    ready = {}
     done, finished = set(), set()
-    for t, task in enumerate(tasks + [None]):
-        stage(task, previous, t % 2)
-        if previous is not None:
-            done.add(previous)
-            for g in range(groups):
-                for k in reversed(range(chunks)):
-                    if (1, g, 0) in done and (0, g, k) in done and (g, k) not in finished:
-                        finished.add((g, k))
-                        finish(g, k)
-        previous = task
+    for t, task in enumerate(tasks):
+        done.add(task)
+        for g in range(groups):
+            for k in reversed(range(chunks)):
+                if k > 0 and (1, g, 0) in done and (0, g, k) in done and (g, k) not in finished:
+                    finished.add((g, k))
+                    ready.setdefault(t, []).append((g, k))
+
+    def settle(t):
+        if tasks[t][0] == 1:
+            pack_branch(tasks[t][1])
+        for g, k in ready.get(t, ()):
+            finish(g, k)
+
+    copies[0].wait()
+    load_query(0)
+    stage(0, True, False, False)
+    copies[1].wait()
+
+    def step(t, carry):
+        for i in range(1, last):
+            pl.when(t == i)(functools.partial(load_query, i))
+        fence_here()
+        stage(t, True, True, True)
+        for i in range(1, last):
+            if tasks[i - 1][0] == 1 or ready.get(i - 1):
+                pl.when(t == i)(functools.partial(settle, i - 1))
+        return carry
+
+    lax.fori_loop(1, last, step, 0)
+    stage(last, False, True, False)
+    settle(last - 1)
+    for g in range(groups):
+        finish(g, 0)
     for g in range(groups):
         collect(g)
     for copy in q_copies.values():
@@ -294,15 +326,13 @@
         out_specs=vmem,
         scratch_shapes=[
             pltpu.VMEM((n, rows, groups * PER * HD), BF),
-            pltpu.VMEM((2, tokens, width), BF),
-            pltpu.VMEM((2, tokens, width), BF),
-            pltpu.VMEM((groups, HD, tokens), BF),
-            pltpu.VMEM((tokens, cols), F32),
+            pltpu.VMEM((cols, HD), BF),
+            pltpu.VMEM((2, tokens, groups * HD), BF),
+            pltpu.VMEM((2, tokens, groups * HD), BF),
             pltpu.VMEM((tokens, cols), F32),
             pltpu.VMEM((CHAIN, cols), F32),
-            pltpu.VMEM((CHAIN, cols), F32),
-            pltpu.VMEM((groups, chunks, HD + STAT, cols), F32),
-            pltpu.VMEM((groups, chunks, 8, cols), F32),
+            pltpu.VMEM((groups * (chunks + 1), HD + STAT, cols), F32),
+            pltpu.VMEM((groups * (chunks + 1), 8, cols), F32),
             pltpu.VMEM((groups, 2 * HD + STAT, cols), BF),
             pltpu.VMEM((n, cols, part), BF),
             pltpu.VMEM((1, all_rows), jnp.int32),

time: 18.8 us -> 18.8 us (level)
  no operation moved by 1% of the time
where the time goes in v3:
time: 18.8 us; the launch traced here: 18.6 us
  Pallas kernels  17.3 us (92%)
  between operations  0.66 us (4%)
  local copies, waits for them, and re-layouts  0.63 us (3%)
    pallas_call x1, Pallas kernels, on_device(): pl.pallas_call(functools.partial(kernel, n, rows, tokens, groups, tb), ou...  17.3 us
    unnamed x1, local copies, waits for them, and re-layouts  0.63 us

profile of v3, /device:TPU:0, one launch (start us, length us, event | category | flops | bytes accessed | tf_op | source)
XLA Modules:
  0.0 18.6 jit_solution(13762876306541703466)
XLA Ops:
  0.7 17.3 %cascade.1 = bf16[16,2048]{1,0:T(8,128)(2,1)S(1)} custom-call(bf16[16,2048]{1,0:T(8,128)(2,1)} %q_ref.1, s32[1,64]{1,0:T(1,128)} %bitcast.1, s32[1]{0:T(128)S(6)} %copy.10.len_ref, bf16[4096,256]{1,0:T(8,128)(2,1)} %rk_ref.1, bf16[4096,256]{1,0:T(8,128)(2,1)} %rv_ref.1, bf16[1,4096,256]{2,1,0:T(8,128)(2,1)} %bk_ref.1, bf16[1,4096,256]{2,1,0:T(8,128)(2,1)} %bv_ref.1), custom_call_target="tpu_custom_call" | custom-call | tf_op jit(solution)/shard_map/cascade/pallas_call | solution.py:322
  18.0 0.6 %copy.9 = bf16[16,2048]{1,0:T(8,128)(2,1)} copy(bf16[16,2048]{1,0:T(8,128)(2,1)S(1)} %cascade.1) | data formatting | bytes 131072

commit v4 on v2

--- a/solution.py
+++ b/solution.py
@@ -40,6 +40,7 @@
     cols = slots * PER
     part = rows * PER
     chunks = n // 2
+    span = min(512, tokens)
     all_rows = n * rows
     sbufs, mbufs = (sbuf0, sbuf1), (mbuf0, mbuf1)
     factor = math.log2(math.e) / math.sqrt(HD)
@@ -230,6 +231,46 @@
             copy.start()
             sent.append((g, off, copy))
 
+    def last_stage(g, k, other):
+        for off in (2 * k, 2 * k + 1):
+            peer = me ^ off
+            lanes = pl.ds(pl.multiple_of(lax.rem(peer, 2) * part, part), part)
+            r_top = jnp.max(mbufs[other][:, lanes], axis=0, keepdims=True) * factor
+            top = jnp.broadcast_to(r_top, (8, part))
+            total = jnp.zeros((HD + STAT, part), F32)
+            for start in range(0, tokens, span):
+                tile = slice(start, start + span)
+                s2 = sbufs[other][tile, lanes].reshape(span // 8, 8, part)
+                weights = jnp.exp2(s2 * factor - top[None]).reshape(span, part).astype(BF)
+                left = jnp.concatenate([vt[g, :, tile], jnp.ones((STAT, span), BF)], axis=0)
+                total = total + jnp.dot(left, weights, preferred_element_type=F32)
+            e = place_e[peer]
+            has = jnp.sum(e.astype(F32), axis=0, keepdims=True) > 0.5
+            back = jnp.dot(right[g], e, preferred_element_type=F32)
+            b_num = back[:HD] + back[HD:2 * HD]
+            b_tot = back[2 * HD:2 * HD + 1] + back[2 * HD + 1:2 * HD + 2]
+            b_top = back[2 * HD + 2:2 * HD + 3] + back[2 * HD + 3:2 * HD + 4] + back[2 * HD + 4:2 * HD + 5]
+            b_top = jnp.where(has, b_top, NEG)
+            peak = jnp.maximum(r_top, b_top)
+            x = jnp.exp2(r_top - peak)
+            y = jnp.exp2(b_top - peak)
+            tot = total[HD:HD + 1] * x + b_tot * y
+            inverse = 1.0 / tot
+            out = (total[:HD] * (x * inverse) + b_num * (y * inverse)).astype(BF)
+            lse = split(peak + jnp.log2(tot), 3)
+            lse = jnp.concatenate(lse + [jnp.zeros((1, part), BF)] * (STAT - 3), axis=0)
+            send[g, off, :HD] = out
+            send[g, off, HD:] = lse
+            copy = pltpu.make_async_remote_copy(
+                src_ref=send.at[g, off], dst_ref=recv.at[g, off],
+                send_sem=o_send.at[g, off], recv_sem=o_recv.at[g, off],
+                device_id={"branch": peer}, device_id_type=MESH,
+            )
+            copy.start()
+            sent.append((g, off, copy))
+            pl.semaphore_signal(fence, inc=1)
+            pl.semaphore_wait(fence, 1)
+
     def collect(g):
         blocks_in = [send[g, lax.rem(me, 2)]]
         for gg, off, copy in sent:
@@ -254,15 +295,24 @@
     previous = None
     done, finished = set(), set()
     for t, task in enumerate(tasks + [None]):
-        stage(task, previous, t % 2)
+        if task is None and previous[2] > 0:
+            src, g, k = previous
+            pl.semaphore_signal(fence, inc=1)
+            pl.semaphore_wait(fence, 1)
+            finished.add((g, k))
+            last_stage(g, k, 1 - t % 2)
+        else:
+            stage(task, previous, t % 2)
         if previous is not None:
             done.add(previous)
             for g in range(groups):
                 for k in reversed(range(chunks)):
-                    if (1, g, 0) in done and (0, g, k) in done and (g, k) not in finished:
+                    if k > 0 and (1, g, 0) in done and (0, g, k) in done and (g, k) not in finished:
                         finished.add((g, k))
                         finish(g, k)
         previous = task
+    for g in range(groups):
+        finish(g, 0)
     for g in range(groups):
         collect(g)
     for copy in q_copies.values():

time: 18.8 us -> 18.2 us (0.968)
  Pallas kernels: 17.4 us -> 16.7 us
    pallas_call x1, Pallas kernels: 17.4 us -> 16.7 us  [on_device(): pl.pallas_call(functools.partial(kernel, n, rows, tokens, groups, tb), ou...]
where the time goes in v4:
time: 18.2 us; the launch traced here: 18 us
  Pallas kernels  16.7 us (92%)
  between operations  0.66 us (4%)
  local copies, waits for them, and re-layouts  0.63 us (3%)
    pallas_call x1, Pallas kernels, on_device(): pl.pallas_call(functools.partial(kernel, n, rows, tokens, groups, tb), ou...  16.7 us
    unnamed x1, local copies, waits for them, and re-layouts  0.63 us

profile of v4, /device:TPU:0, one launch (start us, length us, event | category | flops | bytes accessed | tf_op | source)
XLA Modules:
  0.0 18.0 jit_solution(12051196702963397864)
XLA Ops:
  0.7 16.7 %cascade.1 = bf16[16,2048]{1,0:T(8,128)(2,1)S(1)} custom-call(bf16[16,2048]{1,0:T(8,128)(2,1)} %q_ref.1, s32[1,64]{1,0:T(1,128)} %bitcast.1, s32[1]{0:T(128)S(6)} %copy.10.len_ref, bf16[4096,256]{1,0:T(8,128)(2,1)} %rk_ref.1, bf16[4096,256]{1,0:T(8,128)(2,1)} %rv_ref.1, bf16[1,4096,256]{2,1,0:T(8,128)(2,1)} %bk_ref.1, bf16[1,4096,256]{2,1,0:T(8,128)(2,1)} %bv_ref.1), custom_call_target="tpu_custom_call" | custom-call | tf_op jit(solution)/shard_map/cascade/pallas_call | solution.py:340
  17.4 0.6 %copy.9 = bf16[16,2048]{1,0:T(8,128)(2,1)} copy(bf16[16,2048]{1,0:T(8,128)(2,1)S(1)} %cascade.1) | data formatting | bytes 131072

commit v5 on v4

--- a/solution.py
+++ b/solution.py
@@ -31,7 +31,7 @@
 def kernel(
     n, rows, tokens, groups, tb,
     q_ref, rb_ref, len_ref, rk_ref, rv_ref, bk_ref, bv_ref, out_ref,
-    qall, kbuf, vbuf, vt, sbuf0, sbuf1, mbuf0, mbuf1, rnum, rm, right, place_e, rbuf, lbuf,
+    qall, kbuf, vbuf, vt, bias, sbuf0, sbuf1, mbuf0, mbuf1, rnum, rm, right, place_e, rbuf, lbuf,
     send, recv,
     kv_sem, small_sem, fence, q_send, q_recv, o_send, o_recv,
 ):
@@ -90,14 +90,14 @@
         wide = jnp.dot(picker, spread, preferred_element_type=F32)
         wide = jnp.concatenate([wide] * PER, axis=0)
         place_e[d] = jnp.where(same, wide, 0.0).astype(BF)
-    length = jnp.full((8, cols), lbuf[0], jnp.int32)
+    length = jnp.full((tb, HD), lbuf[0], jnp.int32)
 
     own.wait()
     pl.semaphore_wait(barrier, n - 1)
 
     q_copies = {}
     for g in range(groups):
-        for off in range(1, n):
+        for off in reversed(range(1, n)):
             peer = me ^ off
             lanes = pl.ds(g * PER * HD, PER * HD)
             copy = pltpu.make_async_remote_copy(
@@ -109,6 +109,10 @@
             q_copies[g, off] = copy
     copies[2].start()
     copies[3].start()
+
+    for start in range(0, tokens, tb):
+        place = start + lax.broadcasted_iota(jnp.int32, (tb, HD), 0)
+        bias[start:start + tb] = jnp.where(place < length, 0.0, NEG)
 
     def stack(q):
         return jnp.concatenate([q[:, p * HD:(p + 1) * HD] for p in range(PER)], axis=0)
@@ -164,9 +168,9 @@
                 score = lax.dot_general(keys, query, SPLIT_DIMS, preferred_element_type=F32)
                 score = score.reshape(tb // 8, 8, cols)
                 if src == 1:
-                    place = start + 8 * lax.broadcasted_iota(jnp.int32, (tb // 8, 8, cols), 0)
-                    place = place + lax.broadcasted_iota(jnp.int32, (tb // 8, 8, cols), 1)
-                    score = jnp.where(place < length[None], score, NEG)
+                    hide = bias[tile]
+                    hide = jnp.concatenate([hide] * (cols // HD), axis=1)
+                    score = score + hide.reshape(tb // 8, 8, cols)
                 run = jnp.maximum(run, jnp.max(score.reshape(tb // CHAIN, CHAIN, cols), axis=0))
                 sbufs[slot][tile] = score.reshape(tb, cols)
             if second is not None:
@@ -347,6 +351,7 @@
             pltpu.VMEM((2, tokens, width), BF),
             pltpu.VMEM((2, tokens, width), BF),
             pltpu.VMEM((groups, HD, tokens), BF),
+            pltpu.VMEM((tokens, HD), F32),
             pltpu.VMEM((tokens, cols), F32),
             pltpu.VMEM((tokens, cols), F32),
             pltpu.VMEM((CHAIN, cols), F32),

time: 18.2 us -> 17.5 us (0.962)
  Pallas kernels: 16.7 us -> 16.1 us
    pallas_call x1, Pallas kernels: 16.7 us -> 16.1 us  [on_device(): pl.pallas_call(functools.partial(kernel, n, rows, tokens, groups, tb), ou...]
where the time goes in v5:
time: 17.5 us; the launch traced here: 17.4 us
  Pallas kernels  16.1 us (92%)
  between operations  0.66 us (4%)
  local copies, waits for them, and re-layouts  0.63 us (4%)
    pallas_call x1, Pallas kernels, on_device(): pl.pallas_call(functools.partial(kernel, n, rows, tokens, groups, tb), ou...  16.1 us
    unnamed x1, local copies, waits for them, and re-layouts  0.63 us

profile of v5, /device:TPU:0, one launch (start us, length us, event | category | flops | bytes accessed | tf_op | source)
XLA Modules:
  0.0 17.4 jit_solution(703125677285236595)
XLA Ops:
  0.7 16.1 %cascade.1 = bf16[16,2048]{1,0:T(8,128)(2,1)S(1)} custom-call(bf16[16,2048]{1,0:T(8,128)(2,1)} %q_ref.1, s32[1,64]{1,0:T(1,128)} %bitcast.1, s32[1]{0:T(128)S(6)} %copy.10.len_ref, bf16[4096,256]{1,0:T(8,128)(2,1)} %rk_ref.1, bf16[4096,256]{1,0:T(8,128)(2,1)} %rv_ref.1, bf16[1,4096,256]{2,1,0:T(8,128)(2,1)} %bk_ref.1, bf16[1,4096,256]{2,1,0:T(8,128)(2,1)} %bv_ref.1), custom_call_target="tpu_custom_call" | custom-call | tf_op jit(solution)/shard_map/cascade/pallas_call | solution.py:344
  16.7 0.6 %copy.9 = bf16[16,2048]{1,0:T(8,128)(2,1)} copy(bf16[16,2048]{1,0:T(8,128)(2,1)S(1)} %cascade.1) | data formatting | bytes 131072

commit v6 on v5

--- a/solution.py
+++ b/solution.py
@@ -45,6 +45,11 @@
     sbufs, mbufs = (sbuf0, sbuf1), (mbuf0, mbuf1)
     factor = math.log2(math.e) / math.sqrt(HD)
 
+    barrier = pltpu.get_barrier_semaphore()
+    for off in reversed(range(1, n)):
+        peer = me ^ off
+        pl.semaphore_signal(barrier, inc=1, device_id={"branch": peer}, device_id_type=MESH)
+
     copies = [
         pltpu.make_async_copy(src, dst, kv_sem.at[i])
         for i, (src, dst) in enumerate((
@@ -60,10 +65,6 @@
     len_copy.start()
     copies[0].start()
 
-    barrier = pltpu.get_barrier_semaphore()
-    for off in range(1, n):
-        peer = me ^ off
-        pl.semaphore_signal(barrier, inc=1, device_id={"branch": peer}, device_id_type=MESH)
     copies[1].start()
     rb_copy.wait()
     len_copy.wait()

time: 17.5 us -> 17.5 us (level)
  no operation moved by 1% of the time
where the time goes in v6:
time: 17.5 us; the launch traced here: 17.4 us
  Pallas kernels  16.1 us (92%)
  between operations  0.66 us (4%)
  local copies, waits for them, and re-layouts  0.63 us (4%)
    pallas_call x1, Pallas kernels, on_device(): pl.pallas_call(functools.partial(kernel, n, rows, tokens, groups, tb), ou...  16.1 us
    unnamed x1, local copies, waits for them, and re-layouts  0.63 us

profile of v6, /device:TPU:0, one launch (start us, length us, event | category | flops | bytes accessed | tf_op | source)
XLA Modules:
  0.0 17.4 jit_solution(11258278192794497027)
XLA Ops:
  0.7 16.1 %cascade.1 = bf16[16,2048]{1,0:T(8,128)(2,1)S(1)} custom-call(bf16[16,2048]{1,0:T(8,128)(2,1)} %q_ref.1, s32[1,64]{1,0:T(1,128)} %bitcast.1, s32[1]{0:T(128)S(6)} %copy.10.len_ref, bf16[4096,256]{1,0:T(8,128)(2,1)} %rk_ref.1, bf16[4096,256]{1,0:T(8,128)(2,1)} %rv_ref.1, bf16[1,4096,256]{2,1,0:T(8,128)(2,1)} %bk_ref.1, bf16[1,4096,256]{2,1,0:T(8,128)(2,1)} %bv_ref.1), custom_call_target="tpu_custom_call" | custom-call | tf_op jit(solution)/shard_map/cascade/pallas_call | solution.py:345
  16.7 0.6 %copy.9 = bf16[16,2048]{1,0:T(8,128)(2,1)} copy(bf16[16,2048]{1,0:T(8,128)(2,1)S(1)} %cascade.1) | data formatting | bytes 131072
